TPU v7x, 256 devices: a whole 4x4x8 slice. The times are simulated.
256 devices in a mesh: wide: 32 (over y_hi, z, core), narrow: 8 (over x, y_lo).
Axes of the slice: x: 4, y: 4 (y_hi: 2, y_lo: 2; y = y_hi * 2 + y_lo), z: 8, core: 2. Of those that a mesh axis runs over, the one named last changes fastest.
Arguments:
- matrix: float32 [16384, 16384], P('narrow', 'wide'), may hold values from -64 to 64
Outputs:
- rotated: float32 [16384, 16384], P('narrow', 'wide')
All inputs are finite; a program needn't handle non-finite values.
Results may differ from a plain program's by a relative error of at most 0.0003.
Values sent between devices are 32-bit elements; how exact they have to be, the bound alone decides.
No kernel may reach another device: no remote copies, remote signals or barrier semaphores. Data moves between devices by JAX's collectives and lax.ppermute only.
A program may use at most 64 MiB of HBM per device.

v0:
```python
import jax
import jax.numpy as jnp
from jax import lax
from jax.sharding import PartitionSpec as P

STEPS = 2


def from_behind(value, axis, steps):
    count = lax.axis_size(axis)
    pairs = [(source, (source + steps) % count) for source in range(count)]
    return lax.ppermute(value, axis, pairs)


def product(left, right):
    return jnp.dot(left, right, precision=lax.Precision.HIGHEST)


def spd_solve(factor_low, right_side):
    first_pass = lax.linalg.triangular_solve(factor_low, right_side, left_side=True, lower=True)
    return lax.linalg.triangular_solve(
        factor_low, first_pass, left_side=True, lower=True, transpose_a=True
    )


def turn_pair(upper_block, lower_block, cross_gram, upper_norms, lower_norms):
    damped = cross_gram / (upper_norms[:, None] + lower_norms[None, :])
    block_width = damped.shape[0]
    identity = jnp.eye(block_width, dtype=damped.dtype)
    left_square = product(damped, damped.T)
    left_factor = jnp.linalg.cholesky(identity + left_square)
    solved = spd_solve(left_factor, jnp.concatenate([identity, damped], axis=1))
    inverse = solved[:, :block_width]
    inverse_damped = solved[:, block_width:]
    keep_upper = 2.0 * inverse - identity
    into_lower = 2.0 * inverse_damped
    into_upper = -2.0 * inverse_damped.T
    keep_lower = identity - 2.0 * product(damped.T, inverse_damped)
    new_upper = product(upper_block, keep_upper) + product(lower_block, into_upper)
    new_lower = product(upper_block, into_lower) + product(lower_block, keep_lower)
    return (new_upper, new_lower)


def gram_terms(upper_block, pieces):
    block_width = upper_block.shape[1]
    whole_pair = jnp.concatenate((upper_block,) + pieces, axis=1)
    summed = lax.psum(product(whole_pair.T, whole_pair), "narrow")
    diagonal = jnp.diagonal(summed)
    return (summed[:block_width, block_width:], diagonal[:block_width], diagonal[block_width:])


def move_lower(lower_block):
    return (from_behind(lower_block, "wide", 1),)


def shards(matrix):
    block_width = matrix.shape[1] // 2
    upper_block = matrix[:, :block_width]
    pieces = (matrix[:, block_width:],)
    for step_index in range(STEPS):
        cross_gram, upper_norms, lower_norms = gram_terms(upper_block, pieces)
        lower_block = pieces[0]
        upper_block, lower_block = turn_pair(
            upper_block, lower_block, cross_gram, upper_norms, lower_norms
        )
        pieces = move_lower(lower_block)
    return jnp.concatenate((upper_block,) + pieces, axis=1)


def solution(mesh):
    in_specs = (P("narrow", "wide"),)
    out_specs = P("narrow", "wide")
    return jax.shard_map(shards, mesh=mesh, in_specs=in_specs, out_specs=out_specs, check_vma=False)
```

profile of v0, /device:TPU:16, one launch (start us, length us, event | category | flops | bytes accessed | tf_op | source)
XLA Modules:
  0.0 424.8 jit_solution(5533521235223102054)
XLA Ops:
  6.5 11.2 %fusion.69 = f32[512,512]{0,1:T(8,128)} fusion(f32[2048,512]{1,0:T(8,128)} %param.6), kind=kOutput, calls=%fused_computation.131 | convolution fusion | flops 6442450944 | bytes 5242880 | tf_op jit(solution)/shard_map/dot_general | solution.py:16
  18.1 85.3 %all-reduce.4.cloned.1.call-done = f32[512,512]{0,1:T(8,128)} async-done(((f32[512,512]{0,1:T(8,128)}), f32[512,512]{0,1:T(8,128)}) %all-reduce.4.cloned.1.call-update) | async-done | bytes 1048592 | tf_op jit(solution)/shard_map/psum | solution.py:47
  103.4 8.4 %gather_fusion = f32[512]{0:T(512)S(1)} fusion(f32[512,512]{0,1:T(8,128)} %all-reduce.4.cloned.1.call-done, s32[512]{0:T(512)S(1)} %bitcast.100), kind=kCustom, calls=%fused_computation | custom fusion | bytes 8192 | tf_op jit(solution)/shard_map/jit(diagonal)/cond/branch_0_fun/gather | solution.py:48
  113.7 11.7 %cholesky.130 = f32[128,128]{1,0:T(8,128)S(1)} custom-call(f32[128,128]{1,0:T(8,128)S(1)} %cholesky.194), custom_call_target="Cholesky" | custom-call | tf_op jit(solution)/shard_map/jit(cholesky)/cholesky | solution.py:31
  125.4 9.8 %custom-call.21 = f32[1,128,128]{1,2,0:T(8,128)S(1)} custom-call(f32[1,128,128]{2,1,0:T(8,128)S(1)} %get-tuple-element.67), custom_call_target="InvertDiagBlocksLowerTriangular" | custom-call | tf_op jit(solution)/shard_map/jit(cholesky)/cholesky | solution.py:31
  135.8 11.7 %cholesky.147 = f32[128,128]{1,0:T(8,128)S(1)} custom-call(f32[128,128]{1,0:T(8,128)S(1)} %convolution_subtract_fusion.5), custom_call_target="Cholesky" | custom-call | tf_op jit(solution)/shard_map/jit(cholesky)/cholesky | solution.py:31
  149.5 3.8 while.8
  153.3 20.2 %custom-call.23 = f32[2,128,128]{1,2,0:T(8,128)S(1)} custom-call(f32[2,128,128]{2,1,0:T(8,128)S(1)} %get-tuple-element.37), custom_call_target="InvertDiagBlocksLowerTriangular" | custom-call | tf_op jit(solution)/shard_map/triangular_solve/custom-call.4 | solution.py:21
  176.9 3.7 fusion.7
  180.6 2.1 fusion.4
  184.9 3.6 convolution_add_fusion.3
  188.6 23.5 %collective-permute-done = f32[2048,256]{0,1:T(8,128)S(1)} collective-permute-done((f32[2048,256]{0,1:T(8,128)S(1)}, f32[2048,256]{0,1:T(8,128)S(1)}, u32[]{:S(2)}, u32[]{:S(2)}) %collective-permute-start) | collective-permute-done | bytes 2097184 | tf_op jit(solution)/shard_map/ppermute | solution.py:12
  213.4 8.2 %fusion = f32[512,512]{0,1:T(8,128)} fusion(f32[2048,256]{0,1:T(8,128)S(1)} %collective-permute-done, f32[2048,256]{0,1:T(8,128)S(1)} %bitcast.102), kind=kOutput, calls=%fused_computation.6 | convolution fusion | flops 6443499520 | bytes 5242880 | tf_op jit(solution)/shard_map/dot_general | solution.py:16
  221.6 80.6 %all-reduce.6.cloned.1.call-done = f32[512,512]{0,1:T(8,128)} async-done(((f32[512,512]{0,1:T(8,128)}), f32[512,512]{0,1:T(8,128)}) %all-reduce.6.cloned.1.call-update) | async-done | bytes 1048592 | tf_op jit(solution)/shard_map/psum | solution.py:47
  302.2 8.4 %gather_fusion.1 = f32[512]{0:T(512)S(1)} fusion(f32[512,512]{0,1:T(8,128)} %all-reduce.6.cloned.1.call-done, s32[512]{0:T(512)S(1)} %bitcast.101), kind=kCustom, calls=%fused_computation.1 | custom fusion | bytes 8192 | tf_op jit(solution)/shard_map/jit(diagonal)/cond/branch_0_fun/gather | solution.py:48
  312.5 11.7 %cholesky.164 = f32[128,128]{1,0:T(8,128)S(1)} custom-call(f32[128,128]{1,0:T(8,128)S(1)} %cholesky.197), custom_call_target="Cholesky" | custom-call | tf_op jit(solution)/shard_map/jit(cholesky)/cholesky | solution.py:31
  325.0 9.8 %custom-call.24 = f32[1,128,128]{1,2,0:T(8,128)S(1)} custom-call(f32[1,128,128]{2,1,0:T(8,128)S(1)} %get-tuple-element.63), custom_call_target="InvertDiagBlocksLowerTriangular" | custom-call | tf_op jit(solution)/shard_map/jit(cholesky)/cholesky | solution.py:31
  335.3 11.7 %cholesky.181 = f32[128,128]{1,0:T(8,128)S(1)} custom-call(f32[128,128]{1,0:T(8,128)S(1)} %convolution_subtract_fusion.4), custom_call_target="Cholesky" | custom-call | tf_op jit(solution)/shard_map/jit(cholesky)/cholesky | solution.py:31
  349.0 4.1 while.9
  353.1 20.1 %custom-call.26 = f32[2,128,128]{1,2,0:T(8,128)S(1)} custom-call(f32[2,128,128]{2,1,0:T(8,128)S(1)} %get-tuple-element.39), custom_call_target="InvertDiagBlocksLowerTriangular" | custom-call | tf_op jit(solution)/shard_map/triangular_solve/custom-call.4 | solution.py:21
  383.0 2.1 convolution_add_fusion.1
  385.1 24.9 %collective-permute-done.1 = f32[2048,256]{0,1:T(8,128)S(1)} collective-permute-done((f32[2048,256]{0,1:T(8,128)S(1)}, f32[2048,256]{0,1:T(8,128)S(1)}, u32[]{:S(2)}, u32[]{:S(2)}) %collective-permute-start.1) | collective-permute-done | bytes 2097184 | tf_op jit(solution)/shard_map/ppermute | solution.py:12
  410.0 2.4 pad_maximum_fusion
  412.4 5.3 %copy.27 = f32[2048,512]{1,0:T(8,128)} copy(f32[2048,512]{0,1:T(8,128)} %pad_maximum_fusion) | data formatting | bytes 8388608 | tf_op jit(solution)/shard_map/concatenate | solution.py:67
  (77 shorter events, 31.8 us)
Async XLA Ops:
  6.5 96.8 %all-reduce.4.cloned.1.call-start = ((), (), s32[]{:S(2)}) async-start(), calls=%async_computation | async-start | bytes 2097152 | tf_op jit(solution)/shard_map/psum | solution.py:47
  17.7 284.5 %all-reduce.6.cloned.1.call-start = ((), (), s32[]{:S(2)}) async-start(), calls=%async_computation.1 | async-start | bytes 2097152 | tf_op jit(solution)/shard_map/psum | solution.py:47
  176.9 3.7 copy-start
  182.7 29.3 %collective-permute-start = (f32[2048,256]{0,1:T(8,128)S(1)}, f32[2048,256]{0,1:T(8,128)S(1)}, u32[]{:S(2)}, u32[]{:S(2)}) collective-permute-start(f32[2048,256]{0,1:T(8,128)S(1)} %fusion.4), channel_id=1, source_target_pairs={{0,8},{8,16},{16,24},{24,32},{32,40},{40,48},{48,56},{56,64},{64,7... | collective-permute-start | bytes 6291464 | tf_op jit(solution)/shard_map/ppermute | solution.py:12
  212.0 1.3 copy-start.1
  376.5 2.1 copy-start.2
  380.7 29.3 %collective-permute-start.1 = (f32[2048,256]{0,1:T(8,128)S(1)}, f32[2048,256]{0,1:T(8,128)S(1)}, u32[]{:S(2)}, u32[]{:S(2)}) collective-permute-start(f32[2048,256]{0,1:T(8,128)S(1)} %convolution_add_fusion), channel_id=1, source_target_pairs={{0,8},{8,16},{16,24},{24,32},{32,40},{40,48},{48,56},{56,64},{64,7... | collective-permute-start | bytes 6291464 | tf_op jit(solution)/shard_map/ppermute | solution.py:12
Sparse Core Ops, SparseCore 0:
  17.8 85.4 all-reduce.3
  221.7 80.4 all-reduce.5
where the time goes:
time: 429 us; the launch traced here: 425 us
  waiting for transfers between devices  214 us (50%)
  other arithmetic  114 us (27%)
  matrix products  47.5 us (11%)
  local copies, waits for them, and re-layouts  32 us (7%)
  between operations  16.5 us (4%)
    psum x2, waiting for transfers between devices, gram_terms(): summed = lax.psum(product(whole_pair.T, whole_pair), 'narrow')  166 us
    another operation x13, other arithmetic, turn_pair(): left_factor = jnp.linalg.cholesky(identity + left_square)  68.6 us
    ppermute x2, waiting for transfers between devices, from_behind(): return lax.ppermute(value, axis, pairs)  48.4 us
    dot_general x14, matrix products, product(): return jnp.dot(left, right, precision=lax.Precision.HIGHEST)  41 us
    another operation x5, other arithmetic, spd_solve(): lax.linalg.triangular_solve(factor_low, first_pass, left_side=True, lower...  40.3 us
    gather x2, local copies, waits for them, and re-layouts, gram_terms(): diagonal = jnp.diagonal(summed)  16.8 us
  transfers between devices with their start and end apart: 4, of which 4 were waited for; matrix products, arithmetic and copies ran while one was open for 2% of the time, Pallas kernels for 0%

commit v1 on v0

--- a/solution.py
+++ b/solution.py
@@ -44,7 +44,7 @@
 def gram_terms(upper_block, pieces):
     block_width = upper_block.shape[1]
     whole_pair = jnp.concatenate((upper_block,) + pieces, axis=1)
-    summed = lax.psum(product(whole_pair.T, whole_pair), "narrow")
+    summed = jnp.sum(lax.all_gather(product(whole_pair.T, whole_pair), "narrow"), axis=0)
     diagonal = jnp.diagonal(summed)
     return (summed[:block_width, block_width:], diagonal[:block_width], diagonal[block_width:])
 

time: 429 us -> 614 us (1.43)
  waiting for transfers between devices: 214 us -> 393 us
  other arithmetic: 114 us -> 121 us
    all_gather x0 -> x2, waiting for transfers between devices: none -> 345 us  [gram_terms(): lax.all_gather(product(whole_pair.T, whole_pair), 'narrow')]
    psum x2 -> x0, waiting for transfers between devices: 166 us -> none  [gram_terms(): summed = lax.psum(product(whole_pair.T, whole_pair), 'narrow')]
    reduce_sum x0 -> x2, other arithmetic: none -> 9.07 us  [gram_terms(): jnp.sum(lax.all_gather(product(whole_pair.T, whole_pair), 'narrow'), axis=0)]
    gather x2, local copies, waits for them, and re-layouts: 16.8 us -> 9.33 us  [gram_terms(): diagonal = jnp.diagonal(summed)]
where the time goes in v1:
time: 614 us; the launch traced here: 605 us
  waiting for transfers between devices  393 us (64%)
  other arithmetic  121 us (20%)
  matrix products  47.1 us (8%)
  local copies, waits for them, and re-layouts  26.5 us (4%)
  between operations  16.6 us (3%)
    all_gather x2, waiting for transfers between devices, gram_terms(): lax.all_gather(product(whole_pair.T, whole_pair), 'narrow')  345 us
    another operation x13, other arithmetic, turn_pair(): left_factor = jnp.linalg.cholesky(identity + left_square)  68.6 us
    ppermute x2, waiting for transfers between devices, from_behind(): return lax.ppermute(value, axis, pairs)  48.5 us
    dot_general x14, matrix products, product(): return jnp.dot(left, right, precision=lax.Precision.HIGHEST)  40.6 us
    another operation x5, other arithmetic, spd_solve(): lax.linalg.triangular_solve(factor_low, first_pass, left_side=True, lower...  40.3 us
  transfers between devices with their start and end apart: 4, of which 4 were waited for; matrix products, arithmetic and copies ran while one was open for 2% of the time, Pallas kernels for 0%

profile of v1, /device:TPU:16, one launch (start us, length us, event | category | flops | bytes accessed | tf_op | source)
XLA Modules:
  0.0 605.2 jit_solution(1182759146424132403)
XLA Ops:
  6.5 11.1 %fusion.69 = f32[512,512]{1,0:T(8,128)} fusion(f32[2048,512]{1,0:T(8,128)} %param.6), kind=kOutput, calls=%fused_computation.131 | convolution fusion | flops 6442450944 | bytes 5242880 | tf_op jit(solution)/shard_map/dot_general | solution.py:16
  17.7 173.4 %all-gather.5.cloned.1.call-done = f32[4096,512]{1,0:T(8,128)} async-done(((f32[512,512]{1,0:T(8,128)}), f32[4096,512]{1,0:T(8,128)}) %all-gather.5.cloned.1.call-update) | async-done | bytes 8388624 | tf_op jit(solution)/shard_map/all_gather | solution.py:47
  191.2 4.5 reduce_sum.18
  195.7 4.8 gather_fusion
  201.6 11.7 %cholesky.130 = f32[128,128]{1,0:T(8,128)S(1)} custom-call(f32[128,128]{1,0:T(8,128)S(1)} %cholesky.194), custom_call_target="Cholesky" | custom-call | tf_op jit(solution)/shard_map/jit(cholesky)/cholesky | solution.py:31
  213.4 9.8 %custom-call.21 = f32[1,128,128]{1,2,0:T(8,128)S(1)} custom-call(f32[1,128,128]{2,1,0:T(8,128)S(1)} %get-tuple-element.67), custom_call_target="InvertDiagBlocksLowerTriangular" | custom-call | tf_op jit(solution)/shard_map/jit(cholesky)/cholesky | solution.py:31
  223.7 11.7 %cholesky.147 = f32[128,128]{1,0:T(8,128)S(1)} custom-call(f32[128,128]{1,0:T(8,128)S(1)} %convolution_subtract_fusion.5), custom_call_target="Cholesky" | custom-call | tf_op jit(solution)/shard_map/jit(cholesky)/cholesky | solution.py:31
  237.5 4.0 while.8
  241.5 20.2 %custom-call.23 = f32[2,128,128]{1,2,0:T(8,128)S(1)} custom-call(f32[2,128,128]{2,1,0:T(8,128)S(1)} %get-tuple-element.37), custom_call_target="InvertDiagBlocksLowerTriangular" | custom-call | tf_op jit(solution)/shard_map/triangular_solve/custom-call.4 | solution.py:21
  265.1 3.6 fusion.7
  272.9 3.6 convolution_add_fusion.3
  276.5 23.5 %collective-permute-done = f32[2048,256]{0,1:T(8,128)S(1)} collective-permute-done((f32[2048,256]{0,1:T(8,128)S(1)}, f32[2048,256]{0,1:T(8,128)S(1)}, u32[]{:S(2)}, u32[]{:S(2)}) %collective-permute-start) | collective-permute-done | bytes 2097184 | tf_op jit(solution)/shard_map/ppermute | solution.py:12
  301.3 8.2 %fusion = f32[512,512]{1,0:T(8,128)} fusion(f32[2048,256]{0,1:T(8,128)S(1)} %collective-permute-done, f32[2048,256]{0,1:T(8,128)S(1)} %bitcast.104), kind=kOutput, calls=%fused_computation.6 | convolution fusion | flops 6443499520 | bytes 5242880 | tf_op jit(solution)/shard_map/dot_general | solution.py:16
  309.6 171.5 %all-gather.7.cloned.1.call-done = f32[4096,512]{1,0:T(8,128)} async-done(((f32[512,512]{1,0:T(8,128)}), f32[4096,512]{1,0:T(8,128)}) %all-gather.7.cloned.1.call-update) | async-done | bytes 8388624 | tf_op jit(solution)/shard_map/all_gather | solution.py:47
  481.1 4.5 reduce_sum.19
  486.3 4.5 gather_fusion.1
  492.9 11.7 %cholesky.164 = f32[128,128]{1,0:T(8,128)S(1)} custom-call(f32[128,128]{1,0:T(8,128)S(1)} %cholesky.197), custom_call_target="Cholesky" | custom-call | tf_op jit(solution)/shard_map/jit(cholesky)/cholesky | solution.py:31
  504.7 9.8 %custom-call.24 = f32[1,128,128]{1,2,0:T(8,128)S(1)} custom-call(f32[1,128,128]{2,1,0:T(8,128)S(1)} %get-tuple-element.63), custom_call_target="InvertDiagBlocksLowerTriangular" | custom-call | tf_op jit(solution)/shard_map/jit(cholesky)/cholesky | solution.py:31
  514.9 11.7 %cholesky.181 = f32[128,128]{1,0:T(8,128)S(1)} custom-call(f32[128,128]{1,0:T(8,128)S(1)} %convolution_subtract_fusion.4), custom_call_target="Cholesky" | custom-call | tf_op jit(solution)/shard_map/jit(cholesky)/cholesky | solution.py:31
  529.4 4.1 while.9
  533.4 20.1 %custom-call.26 = f32[2,128,128]{1,2,0:T(8,128)S(1)} custom-call(f32[2,128,128]{2,1,0:T(8,128)S(1)} %get-tuple-element.39), custom_call_target="InvertDiagBlocksLowerTriangular" | custom-call | tf_op jit(solution)/shard_map/triangular_solve/custom-call.4 | solution.py:21
  565.4 25.0 %collective-permute-done.1 = f32[2048,256]{0,1:T(8,128)S(1)} collective-permute-done((f32[2048,256]{0,1:T(8,128)S(1)}, f32[2048,256]{0,1:T(8,128)S(1)}, u32[]{:S(2)}, u32[]{:S(2)}) %collective-permute-start.1) | collective-permute-done | bytes 2097184 | tf_op jit(solution)/shard_map/ppermute | solution.py:12
  590.4 2.4 pad_maximum_fusion
  592.8 5.3 copy.59
  (83 shorter events, 35.6 us)
Async XLA Ops:
  6.5 184.6 %all-gather.5.cloned.1.call-start = ((), (), s32[]{:S(2)}) async-start(), calls=%async_computation | async-start | bytes 9437184 | tf_op jit(solution)/shard_map/all_gather | solution.py:47
  17.6 463.5 %all-gather.7.cloned.1.call-start = ((), (), s32[]{:S(2)}) async-start(), calls=%async_computation.1 | async-start | bytes 9437184 | tf_op jit(solution)/shard_map/all_gather | solution.py:47
  265.1 3.7 copy-start
  270.7 29.3 %collective-permute-start = (f32[2048,256]{0,1:T(8,128)S(1)}, f32[2048,256]{0,1:T(8,128)S(1)}, u32[]{:S(2)}, u32[]{:S(2)}) collective-permute-start(f32[2048,256]{0,1:T(8,128)S(1)} %fusion.4), channel_id=1, source_target_pairs={{0,8},{8,16},{16,24},{24,32},{32,40},{40,48},{48,56},{56,64},{64,7... | collective-permute-start | bytes 6291464 | tf_op jit(solution)/shard_map/ppermute | solution.py:12
  300.0 1.3 copy-start.1
  557.0 2.1 copy-start.2
  561.0 29.3 %collective-permute-start.1 = (f32[2048,256]{0,1:T(8,128)S(1)}, f32[2048,256]{0,1:T(8,128)S(1)}, u32[]{:S(2)}, u32[]{:S(2)}) collective-permute-start(f32[2048,256]{0,1:T(8,128)S(1)} %convolution_add_fusion), channel_id=1, source_target_pairs={{0,8},{8,16},{16,24},{24,32},{32,40},{40,48},{48,56},{56,64},{64,7... | collective-permute-start | bytes 6291464 | tf_op jit(solution)/shard_map/ppermute | solution.py:12
Sparse Core Ops, SparseCore 0:
  17.8 173.3 all-gather.4
  309.7 171.3 all-gather.6
